TPU v7x, 32 devices: a whole 2x2x4 slice. The times are simulated.
32 devices in a mesh: grp: 2 (over y), lat: 4 (over z), lay: 4 (over x, core).
Axes of the slice: x: 2, y: 2, z: 4, core: 2. Of those that a mesh axis runs over, the one named last changes fastest.
Arguments:
- acts: bfloat16 [128, 4, 1280], P(('grp', 'lat'), 'lay'), parts along dimension 0, may hold values from -6 to 6
- w_enc: bfloat16 [4, 1280, 1536], P('lay', None, 'lat'), may hold values from -0.078125 to 0.078125
- w_dec: bfloat16 [1536, 4, 1280], P('lat', 'lay'), may hold values from -0.15625 to 0.15625
- b_enc: float32 [1536], P('lat'), may hold values from -3 to 3
- b_dec: float32 [4, 1280], P('lay'), may hold values from -3 to 3
Outputs:
- lat_grad: bfloat16 [128, 1536], P('grp', 'lat'), parts along dimension 0
- enc_grad: bfloat16 [8, 1280, 1536], P(('grp', 'lay'), None, 'lat'), parts along dimension 0
- dec_grad: bfloat16 [1536, 8, 1280], P('lat', ('grp', 'lay')), parts along dimension 1
There are 2 independent parts, one for each index of `grp`. A program takes and returns all parts, laid end to end along the dimension named above; an argument that names none is the same for every part. Nothing has to cross between parts.
All inputs are finite; a program needn't handle non-finite values.
Results may differ from a plain program's by a relative error of at most 0.023.
Values may be sent and summed in bfloat16 or wider, within the bound.
No kernel may reach another device: no remote copies, remote signals or barrier semaphores. Data moves between devices by JAX's collectives and lax.ppermute only.
A program may use at most 64 MiB of HBM per device.

v0:
```python
import jax
import jax.numpy as jnp
from jax import lax
from jax.sharding import PartitionSpec as P


def on_device(acts, w_enc, w_dec, b_enc, b_dec):
    row_dev, lay_dev, width = acts.shape
    lat_dev = w_enc.shape[2]
    gathered = lax.all_gather(acts, "lat", axis=0, tiled=True)
    term = jnp.einsum("bld,ldm->bm", gathered, w_enc, preferred_element_type=jnp.float32)
    pre = lax.psum(term.astype(jnp.bfloat16), "lay").astype(jnp.float32) + b_enc[None, :]
    code = (jax.nn.softplus(4.0 * pre) / 4.0).astype(jnp.bfloat16)
    slope = jax.nn.sigmoid(4.0 * pre)
    w_flat = w_dec.reshape(lat_dev, lay_dev * width)
    mine = lax.psum_scatter(
        jnp.dot(code, w_flat, preferred_element_type=jnp.float32).astype(jnp.bfloat16),
        "lat",
        scatter_dimension=0,
        tiled=True,
    ).astype(jnp.float32)
    recon = mine.reshape(row_dev, lay_dev, width)
    err_own = (recon + b_dec[None, :, :] - acts.astype(jnp.float32)).astype(jnp.bfloat16)
    err_all = lax.all_gather(err_own, "lat", axis=0, tiled=True)
    back = jnp.einsum("bld,mld->bm", err_all, w_dec, preferred_element_type=jnp.float32)
    back_total = lax.psum(back.astype(jnp.bfloat16), "lay").astype(jnp.float32)
    lat_grad = (back_total * slope).astype(jnp.bfloat16)
    enc_grad = jnp.einsum(
        "bld,bm->ldm", gathered, lat_grad, preferred_element_type=jnp.float32
    ).astype(jnp.bfloat16)
    dec_grad = jnp.einsum("bm,bld->mld", code, err_all, preferred_element_type=jnp.float32).astype(
        jnp.bfloat16
    )
    return (lat_grad, enc_grad, dec_grad)


def solution(mesh):
    in_specs = (
        P(("grp", "lat"), "lay", None),
        P("lay", None, "lat"),
        P("lat", "lay", None),
        P("lat"),
        P("lay", None),
    )
    out_specs = (P("grp", "lat"), P(("grp", "lay"), None, "lat"), P("lat", ("grp", "lay"), None))
    return jax.shard_map(
        on_device, mesh=mesh, in_specs=in_specs, out_specs=out_specs, check_vma=False
    )
```

profile of v0, /device:TPU:0, one launch (start us, length us, event | category | flops | bytes accessed | tf_op | source)
XLA Modules:
  0.0 92.7 jit_solution(12890388767885433730)
XLA Ops:
  7.2 0.0 copy-start
  7.2 0.0 copy-start.3
  7.2 0.0 reduce-scatter.2.cloned.1.call-start
  7.2 15.5 %all_gather.6 = bf16[64,1,1280]{2,0,1:T(8,128)(2,1)S(1)} all-gather(bf16[16,1,1280]{2,0,1:T(8,128)(2,1)} %param.5), channel_id=1, replica_groups=mesh['grp'=2,'lat'=4,'lay'=4] {'lat'}, dimensions={0}, use_global_device_ids=true | all-gather | bytes 204800 | tf_op jit(solution)/shard_map/all_gather | solution.py:10
  22.8 1.5 %convolution_convert_fusion.4 = bf16[64,384]{1,0:T(8,128)(2,1)S(1)} fusion(bf16[1,1280,384]{2,1,0:T(8,128)(2,1)} %param.6, bf16[64,1,1280]{2,0,1:T(8,128)(2,1)S(1)} %all_gather.6), kind=kOutput, calls=%fused_computation.6 | convolution fusion | flops 62939136 | bytes 1196032 | tf_op jit(solution)/shard_map/bld,ldm->bm/dot_general | solution.py:11
  24.2 0.0 copy-start.4
  24.3 0.0 copy-start.2
  24.3 10.7 %psum.14 = bf16[64,384]{1,0:T(8,128)(2,1)S(1)} all-reduce(bf16[64,384]{1,0:T(8,128)(2,1)S(1)} %convolution_convert_fusion.4), channel_id=1, replica_groups=mesh['grp'=2,'lat'=4,'lay'=4] {'lay'}, use_global_device_ids=true, to_apply=%region_0.0 | all-reduce | flops 24576 | bytes 98304 | tf_op jit(solution)/shard_map/psum | solution.py:12
  34.9 0.0 copy-done
  34.9 0.0 copy-done.3
  34.9 1.0 %convolution_convert_fusion.2 = bf16[64,1280]{1,0:T(8,128)(2,1)} fusion(bf16[384,1,1280]{2,0,1:T(8,128)(2,1)S(1)} %copy-done, bf16[64,384]{1,0:T(8,128)(2,1)S(1)} %psum.14, f32[384]{0:T(512)S(1)} %copy-done.3), kind=kOutput, calls=%fused_computation.4 | convolution fusion | flops 63266816 | bytes 1197568 | tf_op jit(solution)/shard_map/dot_general | solution.py:17
  35.9 0.0 reduce-scatter.2.cloned.1.call-update
  35.9 0.0 copy-done.4
  36.0 21.4 %reduce-scatter.2.cloned.1.call-done = bf16[16,1280]{1,0:T(8,128)(2,1)} async-done(((bf16[64,1280]{1,0:T(8,128)(2,1)}), bf16[16,1280]{1,0:T(8,128)(2,1)}) %reduce-scatter.2.cloned.1.call-update) | async-done | bytes 40976 | tf_op jit(solution)/shard_map/reduce_scatter | solution.py:16
  57.3 0.0 copy-done.2
  57.3 0.8 fusion.11
  58.1 13.5 %all_gather.7 = bf16[64,1,1280]{2,0,1:T(8,128)(2,1)S(1)} all-gather(bf16[16,1,1280]{2,0,1:T(8,128)(2,1)S(1)} %fusion.11), channel_id=1, replica_groups=mesh['grp'=2,'lat'=4,'lay'=4] {'lat'}, dimensions={0}, use_global_device_ids=true | all-gather | bytes 204800 | tf_op jit(solution)/shard_map/all_gather | solution.py:24
  71.6 0.4 convolution_convert_fusion.3
  72.0 1.4 %fusion.1 = bf16[384,1,1280]{2,0,1:T(8,128)(2,1)} fusion(bf16[64,1,1280]{2,0,1:T(8,128)(2,1)S(1)} %all_gather.7, bf16[64,384]{1,0:T(8,128)(2,1)S(1)} %psum.14, f32[384]{0:T(512)S(1)} %copy-done.3), kind=kOutput, calls=%fused_computation.3 | convolution fusion | flops 63676416 | bytes 1197568 | tf_op jit(solution)/shard_map/bm,bld->mld/dot_general | solution.py:31
  73.5 10.5 %psum.15 = bf16[64,384]{1,0:T(8,128)(2,1)S(1)} all-reduce(bf16[64,384]{1,0:T(8,128)(2,1)S(1)} %convolution_convert_fusion.3), channel_id=1, replica_groups=mesh['grp'=2,'lat'=4,'lay'=4] {'lay'}, use_global_device_ids=true, to_apply=%region_2.3 | all-reduce | flops 24576 | bytes 98304 | tf_op jit(solution)/shard_map/psum | solution.py:26
  84.0 0.0 copy-start.1
  84.1 0.4 fusion
  84.5 1.3 %copy.8 = bf16[1,1280,384]{2,1,0:T(8,128)(2,1)} copy(bf16[1,1280,384]{1,2,0:T(8,128)(2,1)S(1)} %fusion) | data formatting | bytes 1966080
  85.8 0.0 copy-done.1
  (2 shorter events, 0.1 us)
Async XLA Ops:
  7.2 27.8 %copy-start = (bf16[384,1,1280]{2,0,1:T(8,128)(2,1)S(1)}, bf16[384,1,1280]{2,0,1:T(8,128)(2,1)}, u32[]{:S(2)}) copy-start(bf16[384,1,1280]{2,0,1:T(8,128)(2,1)} %param.7) | copy-start | bytes 2949124
  7.2 27.8 %copy-start.3 = (f32[384]{0:T(512)S(1)}, f32[384]{0:T(512)}, u32[]{:S(2)}) copy-start(f32[384]{0:T(512)} %param.8) | copy-start | bytes 4612
  7.2 50.2 %reduce-scatter.2.cloned.1.call-start = ((), (), s32[]{:S(2)}) async-start(), calls=%async_computation.1 | async-start | bytes 204800 | tf_op jit(solution)/shard_map/reduce_scatter | solution.py:16
  24.2 11.7 %copy-start.4 = (f32[1,1280]{1,0:T(1,128)S(1)}, f32[1,1280]{1,0:T(1,128)}, u32[]{:S(2)}) copy-start(f32[1,1280]{1,0:T(1,128)} %param.9) | copy-start | bytes 15364
  24.3 33.1 %copy-start.2 = (bf16[16,1,1280]{2,0,1:T(8,128)(2,1)S(1)}, bf16[16,1,1280]{2,0,1:T(8,128)(2,1)}, u32[]{:S(2)}) copy-start(bf16[16,1,1280]{2,0,1:T(8,128)(2,1)} %param.5) | copy-start | bytes 122884
  84.0 1.8 %copy-start.1 = (bf16[64,384]{1,0:T(8,128)(2,1)}, bf16[64,384]{1,0:T(8,128)(2,1)S(1)}, u32[]{:S(2)}) copy-start(bf16[64,384]{1,0:T(8,128)(2,1)S(1)} %multiply_convert_fusion) | copy-start | bytes 147460
Sparse Core Ops, SparseCore 0:
  36.1 21.2 reduce-scatter.1
where the time goes:
time: 93 us; the launch traced here: 92.7 us
  blocking collectives  50.1 us (54%)
  waiting for transfers between devices  21.4 us (23%)
  between operations  14.1 us (15%)
  matrix products  4.76 us (5%)
  local copies, waits for them, and re-layouts  1.35 us (1%)
    reduce_scatter x1, waiting for transfers between devices, on_device(): lax.psum_scatter(jnp.dot(code, w_flat, preferred_element_type=jnp.float32...  21.4 us
    all_gather x1, blocking collectives, on_device(): gathered = lax.all_gather(acts, 'lat', axis=0, tiled=True)  15.5 us
    all_gather x1, blocking collectives, on_device(): err_all = lax.all_gather(err_own, 'lat', axis=0, tiled=True)  13.5 us
    psum x1, blocking collectives, on_device(): lax.psum(term.astype(jnp.bfloat16), 'lay').astype(jnp.float32)  10.7 us
    psum x1, blocking collectives, on_device(): back_total = lax.psum(back.astype(jnp.bfloat16), 'lay').astype(jnp.float32)  10.5 us
  transfers between devices with their start and end apart: 1, of which 1 were waited for; matrix products, arithmetic and copies ran while one was open for 0% of the time, Pallas kernels for 0%

commit v1 on v0

v1 whole, which is shorter than its diff:
```python
import jax
import jax.numpy as jnp
from jax import lax
from jax.sharding import PartitionSpec as P

DIRECT = 4


def direct(size):
    return size <= DIRECT and size & (size - 1) == 0


def swap(x, axis, size, step):
    return lax.ppermute(x, axis, [(a, a ^ step) for a in range(size)])


def gather_blocks(x, axis, size):
    return [x] + [swap(x, axis, size, k) for k in range(1, size)]


def pair_sum(terms):
    while len(terms) > 1:
        terms = [terms[k] + terms[k + 1] for k in range(0, len(terms), 2)]
    return terms[0]


def all_sum(x, axis, size):
    if not direct(size):
        return lax.psum(x, axis).astype(jnp.float32)
    return pair_sum([t.astype(jnp.float32) for t in gather_blocks(x, axis, size)])


def build(lat, lay):
    def on_device(acts, w_enc, w_dec, b_enc, b_dec):
        row_dev, lay_dev, width = acts.shape
        lat_dev = w_enc.shape[2]
        flat = lay_dev * width
        own = acts.reshape(row_dev, flat)
        we = w_enc.reshape(flat, lat_dev)
        wd = w_dec.reshape(lat_dev, flat)
        bd = b_dec.reshape(1, flat)
        near = direct(lat)
        if near:
            gathered = jnp.concatenate(gather_blocks(own, "lat", lat), axis=0)
        else:
            gathered = lax.all_gather(own, "lat", axis=0, tiled=True)
        term = jnp.dot(gathered, we, preferred_element_type=jnp.float32)
        pre = all_sum(term.astype(jnp.bfloat16), "lay", lay) + b_enc[None, :]
        code = (jax.nn.softplus(4.0 * pre) / 4.0).astype(jnp.bfloat16)
        slope = jax.nn.sigmoid(4.0 * pre)
        part = jnp.dot(code, wd, preferred_element_type=jnp.float32).astype(jnp.bfloat16)
        if near:
            pieces = part.reshape(lat, row_dev, flat)
            mine = pair_sum(
                [pieces[0].astype(jnp.float32)]
                + [swap(pieces[k], "lat", lat, k).astype(jnp.float32) for k in range(1, lat)]
            )
        else:
            mine = lax.psum_scatter(part, "lat", scatter_dimension=0, tiled=True).astype(jnp.float32)
        err_own = (mine + bd - own.astype(jnp.float32)).astype(jnp.bfloat16)
        if near:
            err = jnp.concatenate(gather_blocks(err_own, "lat", lat), axis=0)
        else:
            err = lax.all_gather(err_own, "lat", axis=0, tiled=True)
        back = lax.dot_general(err, wd, (((1,), (1,)), ((), ())), preferred_element_type=jnp.float32)
        total = all_sum(back.astype(jnp.bfloat16), "lay", lay)
        lat_grad = (total * slope).astype(jnp.bfloat16)
        enc_grad = lax.dot_general(
            gathered, lat_grad, (((0,), (0,)), ((), ())), preferred_element_type=jnp.float32
        ).astype(jnp.bfloat16)
        dec_grad = lax.dot_general(
            code, err, (((0,), (0,)), ((), ())), preferred_element_type=jnp.float32
        ).astype(jnp.bfloat16)
        if near:
            me = lax.axis_index("lat")
            blocks = lat_grad.reshape(lat, row_dev, lat_dev)
            lat_grad = jnp.concatenate(
                [lax.dynamic_index_in_dim(blocks, a ^ me, 0, keepdims=False) for a in range(lat)], axis=0
            )
        return (
            lat_grad,
            enc_grad.reshape(lay_dev, width, lat_dev),
            dec_grad.reshape(lat_dev, lay_dev, width),
        )

    return on_device


def solution(mesh):
    in_specs = (
        P(("grp", "lat"), "lay", None),
        P("lay", None, "lat"),
        P("lat", "lay", None),
        P("lat"),
        P("lay", None),
    )
    out_specs = (P("grp", "lat"), P(("grp", "lay"), None, "lat"), P("lat", ("grp", "lay"), None))
    return jax.shard_map(
        build(mesh.shape["lat"], mesh.shape["lay"]),
        mesh=mesh,
        in_specs=in_specs,
        out_specs=out_specs,
        check_vma=False,
    )
```

time: 93 us -> 41.9 us (0.45)
  blocking collectives: 50.1 us -> 0 us
  starting transfers between devices: 0.04 us -> 17.9 us
  between operations: 14.1 us -> 0.75 us
  waiting for transfers between devices: 21.4 us -> 17.2 us
  local copies, waits for them, and re-layouts: 1.35 us -> 0.05 us
    all_gather x2 -> x0, blocking collectives: 29 us -> none  [the longest x1 15.5 us: on_device(): gathered = lax.all_gather(acts, 'lat', axis=0, tiled=True)]
    reduce_scatter x1 -> x0, waiting for transfers between devices: 21.4 us -> none  [on_device(): lax.psum_scatter(jnp.dot(code, w_flat, preferred_element_type=jnp.float32...]
    psum x2 -> x0, blocking collectives: 21.2 us -> none  [the longest x1 10.7 us: on_device(): lax.psum(term.astype(jnp.bfloat16), 'lay').astype(jnp.float32)]
    ppermute x0 -> x15, starting transfers between devices: none -> 17.9 us  [swap(): return lax.ppermute(x, axis, [(a, a ^ step) for a in range(size)])]
    ppermute x0 -> x15, waiting for transfers between devices: none -> 17.2 us  [swap(): return lax.ppermute(x, axis, [(a, a ^ step) for a in range(size)])]
    unnamed x11 -> x8, local copies, waits for them, and re-layouts: 1.35 us -> 0.03 us
  transfers between devices with their start and end apart: 1 -> 15, of which waited for: 1 -> 11; matrix products, arithmetic and copies ran while one was open for 0% -> 3% of each run, Pallas kernels for 0% -> 0%
where the time goes in v1:
time: 41.9 us; the launch traced here: 41.7 us
  starting transfers between devices  17.9 us (43%)
  waiting for transfers between devices  17.2 us (41%)
  matrix products  4.99 us (12%)
  other arithmetic  0.87 us (2%)
  between operations  0.75 us (2%)
    ppermute x15, starting transfers between devices, swap(): return lax.ppermute(x, axis, [(a, a ^ step) for a in range(size)])  17.9 us
    ppermute x15, waiting for transfers between devices, swap(): return lax.ppermute(x, axis, [(a, a ^ step) for a in range(size)])  17.2 us
    dot_general x1, matrix products, on_device(): term = jnp.dot(gathered, we, preferred_element_type=jnp.float32)  1.5 us
    dot_general x1, matrix products, on_device(): lax.dot_general(gathered, lat_grad, (((0,), (0,)), ((), ())), preferred_e...  1.4 us
    dot_general x1, matrix products, on_device(): lax.dot_general(code, err, (((0,), (0,)), ((), ())), preferred_element_ty...  1.39 us
  transfers between devices with their start and end apart: 15, of which 11 were waited for; matrix products, arithmetic and copies ran while one was open for 3% of the time, Pallas kernels for 0%

profile of v1, /device:TPU:0, one launch (start us, length us, event | category | flops | bytes accessed | tf_op | source)
XLA Modules:
  0.0 41.7 jit_solution(2300958929299812644)
XLA Ops:
  0.6 0.0 copy-start
  0.6 0.0 copy-start.2
  0.7 3.1 %collective-permute-start = (bf16[16,1280]{1,0:T(8,128)(2,1)}, bf16[16,1280]{1,0:T(8,128)(2,1)S(1)}, u32[]{:S(2)}, u32[]{:S(2)}) collective-permute-start(bf16[16,1280]{1,0:T(8,128)(2,1)} %bitcast.27), channel_id=1, source_target_pairs={{0,4},{4,0},{8,12},{12,8},{1,5},{5,1},{9,13},{13,9},{2,6},{6,2},{1... | collective-permute-start | bytes 122888 | tf_op jit(solution)/shard_map/ppermute | solution.py:14
  3.8 2.6 %collective-permute-start.1 = (bf16[16,1280]{1,0:T(8,128)(2,1)}, bf16[16,1280]{1,0:T(8,128)(2,1)S(1)}, u32[]{:S(2)}, u32[]{:S(2)}) collective-permute-start(bf16[16,1280]{1,0:T(8,128)(2,1)} %bitcast.28), channel_id=1, source_target_pairs={{0,8},{4,12},{8,0},{12,4},{1,9},{5,13},{9,1},{13,5},{2,10},{6,14},... | collective-permute-start | bytes 122888 | tf_op jit(solution)/shard_map/ppermute | solution.py:14
  6.4 0.0 collective-permute-start.2
  6.4 0.0 collective-permute-done
  6.4 3.3 %collective-permute-done.1 = bf16[16,1280]{1,0:T(8,128)(2,1)S(1)} collective-permute-done((bf16[16,1280]{1,0:T(8,128)(2,1)}, bf16[16,1280]{1,0:T(8,128)(2,1)S(1)}, u32[]{:S(2)}, u32[]{:S(2)}) %collective-permute-start.1) | collective-permute-done | bytes 40992 | tf_op jit(solution)/shard_map/ppermute | solution.py:14
  9.6 2.7 %collective-permute-done.2 = bf16[16,1280]{1,0:T(8,128)(2,1)S(1)} collective-permute-done((bf16[16,1280]{1,0:T(8,128)(2,1)}, bf16[16,1280]{1,0:T(8,128)(2,1)S(1)}, u32[]{:S(2)}, u32[]{:S(2)}) %collective-permute-start.2) | collective-permute-done | bytes 40992 | tf_op jit(solution)/shard_map/ppermute | solution.py:14
  12.4 1.5 %convolution_convert_fusion.4 = bf16[64,384]{1,0:T(8,128)(2,1)S(1)} fusion(bf16[1,1280,384]{2,1,0:T(8,128)(2,1)} %param.6, bf16[16,1280]{1,0:T(8,128)(2,1)S(1)} %collective-permute-done.2, bf16[16,1280]{1,0:T(8,128)(2,1)S(1)} %collective-permute-done.1, bf16[16,1280]{1,0:T(8,128)(2,1)S(1)} %collective-permute-done, bf16[16,1280]{1,0:T(8,128)(2,1)} %bitcast.30), kind=kOutput, calls=%fused_computation.6 | convolution fusion | flops 63594496 | bytes 1196032 | tf_op jit(solution)/shard_map/dot_general | solution.py:47
  13.9 0.0 copy-start.3
  13.9 0.0 copy-start.1
  13.9 0.1 collective-permute-start.3
  14.0 1.6 %collective-permute-start.4 = (bf16[64,384]{1,0:T(8,128)(2,1)S(1)}, bf16[64,384]{1,0:T(8,128)(2,1)S(1)}, u32[]{:S(2)}, u32[]{:S(2)}) collective-permute-start(bf16[64,384]{1,0:T(8,128)(2,1)S(1)} %convolution_convert_fusion.4), channel_id=1, source_target_pairs={{0,2},{1,3},{2,0},{3,1},{4,6},{5,7},{6,4},{7,5},{8,10},{9,11},{10,... | collective-permute-start | bytes 147464 | tf_op jit(solution)/shard_map/ppermute | solution.py:14
  15.5 0.3 collective-permute-start.5
  15.8 0.0 collective-permute-done.3
  15.8 2.3 %collective-permute-done.4 = bf16[64,384]{1,0:T(8,128)(2,1)S(1)} collective-permute-done((bf16[64,384]{1,0:T(8,128)(2,1)S(1)}, bf16[64,384]{1,0:T(8,128)(2,1)S(1)}, u32[]{:S(2)}, u32[]{:S(2)}) %collective-permute-start.4) | collective-permute-done | bytes 49184 | tf_op jit(solution)/shard_map/ppermute | solution.py:14
  18.1 1.1 %collective-permute-done.5 = bf16[64,384]{1,0:T(8,128)(2,1)S(1)} collective-permute-done((bf16[64,384]{1,0:T(8,128)(2,1)S(1)}, bf16[64,384]{1,0:T(8,128)(2,1)S(1)}, u32[]{:S(2)}, u32[]{:S(2)}) %collective-permute-start.5) | collective-permute-done | bytes 49184 | tf_op jit(solution)/shard_map/ppermute | solution.py:14
  19.3 0.0 copy-done.2
  19.3 0.1 fusion.6
  19.4 0.0 copy-done
  19.4 0.3 convolution_convert_fusion.2
  19.7 0.1 collective-permute-start.6
  19.7 1.1 %collective-permute-start.7 = (bf16[16,1280]{1,0:T(8,128)(2,1)S(1)}, bf16[16,1280]{1,0:T(8,128)(2,1)S(1)}, u32[]{:S(2)}, u32[]{:S(2)}) collective-permute-start(bf16[16,1280]{1,0:T(8,128)(2,1)S(1)} %get-tuple-element.5), channel_id=1, source_target_pairs={{0,8},{4,12},{8,0},{12,4},{1,9},{5,13},{9,1},{13,5},{2,10},{6,14},... | collective-permute-start | bytes 122888 | tf_op jit(solution)/shard_map/ppermute | solution.py:14
  20.8 3.3 %collective-permute-start.8 = (bf16[16,1280]{1,0:T(8,128)(2,1)S(1)}, bf16[16,1280]{1,0:T(8,128)(2,1)S(1)}, u32[]{:S(2)}, u32[]{:S(2)}) collective-permute-start(bf16[16,1280]{1,0:T(8,128)(2,1)S(1)} %get-tuple-element.4), channel_id=1, source_target_pairs={{0,12},{4,8},{8,4},{12,0},{1,13},{5,9},{9,5},{13,1},{2,14},{6,10},... | collective-permute-start | bytes 122888 | tf_op jit(solution)/shard_map/ppermute | solution.py:14
  24.1 0.0 copy-done.3
  24.1 0.0 collective-permute-done.6
  24.2 1.5 %collective-permute-done.7 = bf16[16,1280]{1,0:T(8,128)(2,1)S(1)} collective-permute-done((bf16[16,1280]{1,0:T(8,128)(2,1)S(1)}, bf16[16,1280]{1,0:T(8,128)(2,1)S(1)}, u32[]{:S(2)}, u32[]{:S(2)}) %collective-permute-start.7) | collective-permute-done | bytes 40992 | tf_op jit(solution)/shard_map/ppermute | solution.py:14
  25.6 1.0 %collective-permute-done.8 = bf16[16,1280]{1,0:T(8,128)(2,1)S(1)} collective-permute-done((bf16[16,1280]{1,0:T(8,128)(2,1)S(1)}, bf16[16,1280]{1,0:T(8,128)(2,1)S(1)}, u32[]{:S(2)}, u32[]{:S(2)}) %collective-permute-start.8) | collective-permute-done | bytes 40992 | tf_op jit(solution)/shard_map/ppermute | solution.py:14
  26.6 0.0 copy-done.1
  26.7 0.2 collective-permute-start.10
  26.8 3.3 %collective-permute-start.11 = (bf16[16,1280]{1,0:T(8,128)(2,1)S(1)}, bf16[16,1280]{1,0:T(8,128)(2,1)S(1)}, u32[]{:S(2)}, u32[]{:S(2)}) collective-permute-start(bf16[16,1280]{1,0:T(8,128)(2,1)S(1)} %subtract_convert_fusion), channel_id=1, source_target_pairs={{0,12},{4,8},{8,4},{12,0},{1,13},{5,9},{9,5},{13,1},{2,14},{6,10},... | collective-permute-start | bytes 122888 | tf_op jit(solution)/shard_map/ppermute | solution.py:14
  30.1 0.5 %collective-permute-start.9 = (bf16[16,1280]{1,0:T(8,128)(2,1)S(1)}, bf16[16,1280]{1,0:T(8,128)(2,1)S(1)}, u32[]{:S(2)}, u32[]{:S(2)}) collective-permute-start(bf16[16,1280]{1,0:T(8,128)(2,1)S(1)} %subtract_convert_fusion), channel_id=1, source_target_pairs={{0,4},{4,0},{8,12},{12,8},{1,5},{5,1},{9,13},{13,9},{2,6},{6,2},{1... | collective-permute-start | bytes 122888 | tf_op jit(solution)/shard_map/ppermute | solution.py:14
  30.6 1.1 %collective-permute-done.10 = bf16[16,1280]{1,0:T(8,128)(2,1)S(1)} collective-permute-done((bf16[16,1280]{1,0:T(8,128)(2,1)S(1)}, bf16[16,1280]{1,0:T(8,128)(2,1)S(1)}, u32[]{:S(2)}, u32[]{:S(2)}) %collective-permute-start.10) | collective-permute-done | bytes 40992 | tf_op jit(solution)/shard_map/ppermute | solution.py:14
  31.7 1.1 %collective-permute-done.11 = bf16[16,1280]{1,0:T(8,128)(2,1)S(1)} collective-permute-done((bf16[16,1280]{1,0:T(8,128)(2,1)S(1)}, bf16[16,1280]{1,0:T(8,128)(2,1)S(1)}, u32[]{:S(2)}, u32[]{:S(2)}) %collective-permute-start.11) | collective-permute-done | bytes 40992 | tf_op jit(solution)/shard_map/ppermute | solution.py:14
  32.9 1.2 %collective-permute-done.9 = bf16[16,1280]{1,0:T(8,128)(2,1)S(1)} collective-permute-done((bf16[16,1280]{1,0:T(8,128)(2,1)S(1)}, bf16[16,1280]{1,0:T(8,128)(2,1)S(1)}, u32[]{:S(2)}, u32[]{:S(2)}) %collective-permute-start.9) | collective-permute-done | bytes 40992 | tf_op jit(solution)/shard_map/ppermute | solution.py:14
  34.1 0.4 %convolution_convert_fusion.3 = bf16[64,384]{1,0:T(8,128)(2,1)S(1)} fusion(bf16[384,1,1280]{2,0,1:T(8,128)(2,1)S(1)} %copy-done, bf16[16,1280]{1,0:T(8,128)(2,1)S(1)} %collective-permute-done.11, bf16[16,1280]{1,0:T(8,128)(2,1)S(1)} %collective-permute-done.10, bf16[16,1280]{1,0:T(8,128)(2,1)S(1)} %collective-permute-done.9, ...), kind=kOutput, calls=%fused_computation.5 | convolution fusion | flops 63594496 | bytes 1196032 | tf_op jit(solution)/shard_map/dot_general | solution.py:65
  34.5 0.1 collective-permute-start.12
  34.6 1.0 %collective-permute-start.13 = (bf16[64,384]{1,0:T(8,128)(2,1)S(1)}, bf16[64,384]{1,0:T(8,128)(2,1)S(1)}, u32[]{:S(2)}, u32[]{:S(2)}) collective-permute-start(bf16[64,384]{1,0:T(8,128)(2,1)S(1)} %convolution_convert_fusion.3), channel_id=1, source_target_pairs={{0,2},{1,3},{2,0},{3,1},{4,6},{5,7},{6,4},{7,5},{8,10},{9,11},{10,... | collective-permute-start | bytes 147464 | tf_op jit(solution)/shard_map/ppermute | solution.py:14
  35.7 0.8 %collective-permute-start.14 = (bf16[64,384]{1,0:T(8,128)(2,1)S(1)}, bf16[64,384]{1,0:T(8,128)(2,1)S(1)}, u32[]{:S(2)}, u32[]{:S(2)}) collective-permute-start(bf16[64,384]{1,0:T(8,128)(2,1)S(1)} %convolution_convert_fusion.3), channel_id=1, source_target_pairs={{0,3},{1,2},{2,1},{3,0},{4,7},{5,6},{6,5},{7,4},{8,11},{9,10},{10,... | collective-permute-start | bytes 147464 | tf_op jit(solution)/shard_map/ppermute | solution.py:14
  36.5 1.4 %fusion.1 = bf16[384,1,1280]{2,0,1:T(8,128)(2,1)} fusion(bf16[64,384]{1,0:T(8,128)(2,1)S(1)} %fusion.6, bf16[16,1280]{1,0:T(8,128)(2,1)S(1)} %collective-permute-done.11, bf16[16,1280]{1,0:T(8,128)(2,1)S(1)} %collective-permute-done.10, bf16[16,1280]{1,0:T(8,128)(2,1)S(1)} %collective-permute-done.9, bf16[16,1280]{1,0:T(8,128)(2,1)S(1)} %subtract_convert_fusion), kind=kOutput, calls=%fused_computation.3 | convolution fusion | flops 64061440 | bytes 1196032 | tf_op jit(solution)/shard_map/dot_general | solution.py:71
  37.9 0.0 collective-permute-done.12
  37.9 1.0 %collective-permute-done.13 = bf16[64,384]{1,0:T(8,128)(2,1)S(1)} collective-permute-done((bf16[64,384]{1,0:T(8,128)(2,1)S(1)}, bf16[64,384]{1,0:T(8,128)(2,1)S(1)}, u32[]{:S(2)}, u32[]{:S(2)}) %collective-permute-start.13) | collective-permute-done | bytes 49184 | tf_op jit(solution)/shard_map/ppermute | solution.py:14
  38.9 0.7 %collective-permute-done.14 = bf16[64,384]{1,0:T(8,128)(2,1)S(1)} collective-permute-done((bf16[64,384]{1,0:T(8,128)(2,1)S(1)}, bf16[64,384]{1,0:T(8,128)(2,1)S(1)}, u32[]{:S(2)}, u32[]{:S(2)}) %collective-permute-start.14) | collective-permute-done | bytes 49184 | tf_op jit(solution)/shard_map/ppermute | solution.py:14
  39.6 0.1 multiply_convert_fusion
  39.7 0.6 %pad_maximum_fusion.2 = bf16[64,384]{1,0:T(8,128)(2,1)} fusion(bf16[16,384]{1,0:T(8,128)(2,1)S(1)} %get-tuple-element.7, bf16[16,384]{1,0:T(8,128)(2,1)S(1)} %get-tuple-element.8, bf16[16,384]{1,0:T(8,128)(2,1)S(1)} %get-tuple-element.9, bf16[16,384]{1,0:T(8,128)(2,1)S(1)} %get-tuple-element.6), kind=kLoop, calls=%fused_computation.18 | loop fusion | flops 196608 | bytes 98304 | tf_op jit(solution)/shard_map/concatenate | solution.py:77
  40.4 1.4 %fusion = bf16[1,1280,384]{2,1,0:T(8,128)(2,1)} fusion(bf16[64,384]{1,0:T(8,128)(2,1)S(1)} %multiply_convert_fusion, bf16[16,1280]{1,0:T(8,128)(2,1)S(1)} %collective-permute-done.2, bf16[16,1280]{1,0:T(8,128)(2,1)S(1)} %collective-permute-done.1, bf16[16,1280]{1,0:T(8,128)(2,1)S(1)} %collective-permute-done, bf16[16,1280]{1,0:T(8,128)(2,1)S(1)} %bitcast.31), kind=kOutput, calls=%fused_computation.2 | convolution fusion | flops 64061440 | bytes 1196032 | tf_op jit(solution)/shard_map/dot_general | solution.py:68
  (4 shorter events, 0.1 us)
Async XLA Ops:
  0.6 18.7 %copy-start = (bf16[384,1,1280]{2,0,1:T(8,128)(2,1)S(1)}, bf16[384,1,1280]{2,0,1:T(8,128)(2,1)}, u32[]{:S(2)}) copy-start(bf16[384,1,1280]{2,0,1:T(8,128)(2,1)} %param.7) | copy-start | bytes 2949124
  0.6 18.6 %copy-start.2 = (f32[384]{0:T(512)S(1)}, f32[384]{0:T(512)}, u32[]{:S(2)}) copy-start(f32[384]{0:T(512)} %param.8) | copy-start | bytes 4612
  0.7 5.7 %collective-permute-start = (bf16[16,1280]{1,0:T(8,128)(2,1)}, bf16[16,1280]{1,0:T(8,128)(2,1)S(1)}, u32[]{:S(2)}, u32[]{:S(2)}) collective-permute-start(bf16[16,1280]{1,0:T(8,128)(2,1)} %bitcast.27), channel_id=1, source_target_pairs={{0,4},{4,0},{8,12},{12,8},{1,5},{5,1},{9,13},{13,9},{2,6},{6,2},{1... | collective-permute-start | bytes 122888 | tf_op jit(solution)/shard_map/ppermute | solution.py:14
  3.8 5.9 %collective-permute-start.1 = (bf16[16,1280]{1,0:T(8,128)(2,1)}, bf16[16,1280]{1,0:T(8,128)(2,1)S(1)}, u32[]{:S(2)}, u32[]{:S(2)}) collective-permute-start(bf16[16,1280]{1,0:T(8,128)(2,1)} %bitcast.28), channel_id=1, source_target_pairs={{0,8},{4,12},{8,0},{12,4},{1,9},{5,13},{9,1},{13,5},{2,10},{6,14},... | collective-permute-start | bytes 122888 | tf_op jit(solution)/shard_map/ppermute | solution.py:14
  6.4 6.0 %collective-permute-start.2 = (bf16[16,1280]{1,0:T(8,128)(2,1)}, bf16[16,1280]{1,0:T(8,128)(2,1)S(1)}, u32[]{:S(2)}, u32[]{:S(2)}) collective-permute-start(bf16[16,1280]{1,0:T(8,128)(2,1)} %bitcast.29), channel_id=1, source_target_pairs={{0,12},{4,8},{8,4},{12,0},{1,13},{5,9},{9,5},{13,1},{2,14},{6,10},... | collective-permute-start | bytes 122888 | tf_op jit(solution)/shard_map/ppermute | solution.py:14
  13.9 10.2 %copy-start.3 = (f32[1,1280]{1,0:T(1,128)S(1)}, f32[1,1280]{1,0:T(1,128)}, u32[]{:S(2)}) copy-start(f32[1,1280]{1,0:T(1,128)} %param.9) | copy-start | bytes 15364
  13.9 12.7 %copy-start.1 = (bf16[16,1,1280]{2,0,1:T(8,128)(2,1)S(1)}, bf16[16,1,1280]{2,0,1:T(8,128)(2,1)}, u32[]{:S(2)}) copy-start(bf16[16,1,1280]{2,0,1:T(8,128)(2,1)} %param.5) | copy-start | bytes 122884
  13.9 1.9 %collective-permute-start.3 = (bf16[64,384]{1,0:T(8,128)(2,1)S(1)}, bf16[64,384]{1,0:T(8,128)(2,1)S(1)}, u32[]{:S(2)}, u32[]{:S(2)}) collective-permute-start(bf16[64,384]{1,0:T(8,128)(2,1)S(1)} %convolution_convert_fusion.4), channel_id=1, source_target_pairs={{0,1},{1,0},{2,3},{3,2},{4,5},{5,4},{6,7},{7,6},{8,9},{9,8},{10,11... | collective-permute-start | bytes 147464 | tf_op jit(solution)/shard_map/ppermute | solution.py:14
  14.0 4.2 %collective-permute-start.4 = (bf16[64,384]{1,0:T(8,128)(2,1)S(1)}, bf16[64,384]{1,0:T(8,128)(2,1)S(1)}, u32[]{:S(2)}, u32[]{:S(2)}) collective-permute-start(bf16[64,384]{1,0:T(8,128)(2,1)S(1)} %convolution_convert_fusion.4), channel_id=1, source_target_pairs={{0,2},{1,3},{2,0},{3,1},{4,6},{5,7},{6,4},{7,5},{8,10},{9,11},{10,... | collective-permute-start | bytes 147464 | tf_op jit(solution)/shard_map/ppermute | solution.py:14
  15.5 3.7 %collective-permute-start.5 = (bf16[64,384]{1,0:T(8,128)(2,1)S(1)}, bf16[64,384]{1,0:T(8,128)(2,1)S(1)}, u32[]{:S(2)}, u32[]{:S(2)}) collective-permute-start(bf16[64,384]{1,0:T(8,128)(2,1)S(1)} %convolution_convert_fusion.4), channel_id=1, source_target_pairs={{0,3},{1,2},{2,1},{3,0},{4,7},{5,6},{6,5},{7,4},{8,11},{9,10},{10,... | collective-permute-start | bytes 147464 | tf_op jit(solution)/shard_map/ppermute | solution.py:14
  19.7 4.5 %collective-permute-start.6 = (bf16[16,1280]{1,0:T(8,128)(2,1)S(1)}, bf16[16,1280]{1,0:T(8,128)(2,1)S(1)}, u32[]{:S(2)}, u32[]{:S(2)}) collective-permute-start(bf16[16,1280]{1,0:T(8,128)(2,1)S(1)} %get-tuple-element.3), channel_id=1, source_target_pairs={{0,4},{4,0},{8,12},{12,8},{1,5},{5,1},{9,13},{13,9},{2,6},{6,2},{1... | collective-permute-start | bytes 122888 | tf_op jit(solution)/shard_map/ppermute | solution.py:14
  19.7 5.9 %collective-permute-start.7 = (bf16[16,1280]{1,0:T(8,128)(2,1)S(1)}, bf16[16,1280]{1,0:T(8,128)(2,1)S(1)}, u32[]{:S(2)}, u32[]{:S(2)}) collective-permute-start(bf16[16,1280]{1,0:T(8,128)(2,1)S(1)} %get-tuple-element.5), channel_id=1, source_target_pairs={{0,8},{4,12},{8,0},{12,4},{1,9},{5,13},{9,1},{13,5},{2,10},{6,14},... | collective-permute-start | bytes 122888 | tf_op jit(solution)/shard_map/ppermute | solution.py:14
  20.8 5.8 %collective-permute-start.8 = (bf16[16,1280]{1,0:T(8,128)(2,1)S(1)}, bf16[16,1280]{1,0:T(8,128)(2,1)S(1)}, u32[]{:S(2)}, u32[]{:S(2)}) collective-permute-start(bf16[16,1280]{1,0:T(8,128)(2,1)S(1)} %get-tuple-element.4), channel_id=1, source_target_pairs={{0,12},{4,8},{8,4},{12,0},{1,13},{5,9},{9,5},{13,1},{2,14},{6,10},... | collective-permute-start | bytes 122888 | tf_op jit(solution)/shard_map/ppermute | solution.py:14
  26.7 5.1 %collective-permute-start.10 = (bf16[16,1280]{1,0:T(8,128)(2,1)S(1)}, bf16[16,1280]{1,0:T(8,128)(2,1)S(1)}, u32[]{:S(2)}, u32[]{:S(2)}) collective-permute-start(bf16[16,1280]{1,0:T(8,128)(2,1)S(1)} %subtract_convert_fusion), channel_id=1, source_target_pairs={{0,8},{4,12},{8,0},{12,4},{1,9},{5,13},{9,1},{13,5},{2,10},{6,14},... | collective-permute-start | bytes 122888 | tf_op jit(solution)/shard_map/ppermute | solution.py:14
  26.8 6.0 %collective-permute-start.11 = (bf16[16,1280]{1,0:T(8,128)(2,1)S(1)}, bf16[16,1280]{1,0:T(8,128)(2,1)S(1)}, u32[]{:S(2)}, u32[]{:S(2)}) collective-permute-start(bf16[16,1280]{1,0:T(8,128)(2,1)S(1)} %subtract_convert_fusion), channel_id=1, source_target_pairs={{0,12},{4,8},{8,4},{12,0},{1,13},{5,9},{9,5},{13,1},{2,14},{6,10},... | collective-permute-start | bytes 122888 | tf_op jit(solution)/shard_map/ppermute | solution.py:14
  30.1 4.0 %collective-permute-start.9 = (bf16[16,1280]{1,0:T(8,128)(2,1)S(1)}, bf16[16,1280]{1,0:T(8,128)(2,1)S(1)}, u32[]{:S(2)}, u32[]{:S(2)}) collective-permute-start(bf16[16,1280]{1,0:T(8,128)(2,1)S(1)} %subtract_convert_fusion), channel_id=1, source_target_pairs={{0,4},{4,0},{8,12},{12,8},{1,5},{5,1},{9,13},{13,9},{2,6},{6,2},{1... | collective-permute-start | bytes 122888 | tf_op jit(solution)/shard_map/ppermute | solution.py:14
  34.5 3.3 %collective-permute-start.12 = (bf16[64,384]{1,0:T(8,128)(2,1)S(1)}, bf16[64,384]{1,0:T(8,128)(2,1)S(1)}, u32[]{:S(2)}, u32[]{:S(2)}) collective-permute-start(bf16[64,384]{1,0:T(8,128)(2,1)S(1)} %convolution_convert_fusion.3), channel_id=1, source_target_pairs={{0,1},{1,0},{2,3},{3,2},{4,5},{5,4},{6,7},{7,6},{8,9},{9,8},{10,11... | collective-permute-start | bytes 147464 | tf_op jit(solution)/shard_map/ppermute | solution.py:14
  34.6 4.3 %collective-permute-start.13 = (bf16[64,384]{1,0:T(8,128)(2,1)S(1)}, bf16[64,384]{1,0:T(8,128)(2,1)S(1)}, u32[]{:S(2)}, u32[]{:S(2)}) collective-permute-start(bf16[64,384]{1,0:T(8,128)(2,1)S(1)} %convolution_convert_fusion.3), channel_id=1, source_target_pairs={{0,2},{1,3},{2,0},{3,1},{4,6},{5,7},{6,4},{7,5},{8,10},{9,11},{10,... | collective-permute-start | bytes 147464 | tf_op jit(solution)/shard_map/ppermute | solution.py:14
  35.7 3.9 %collective-permute-start.14 = (bf16[64,384]{1,0:T(8,128)(2,1)S(1)}, bf16[64,384]{1,0:T(8,128)(2,1)S(1)}, u32[]{:S(2)}, u32[]{:S(2)}) collective-permute-start(bf16[64,384]{1,0:T(8,128)(2,1)S(1)} %convolution_convert_fusion.3), channel_id=1, source_target_pairs={{0,3},{1,2},{2,1},{3,0},{4,7},{5,6},{6,5},{7,4},{8,11},{9,10},{10,... | collective-permute-start | bytes 147464 | tf_op jit(solution)/shard_map/ppermute | solution.py:14
